TPU v7x, 256 devices: a whole 4x4x8 slice. The times are simulated.
256 devices in a mesh: row: 32 (over z_hi, y, core), col: 8 (over z_lo, x).
Axes of the slice: x: 4, y: 4, z: 8 (z_hi: 4, z_lo: 2; z = z_hi * 2 + z_lo), core: 2. Of those that a mesh axis runs over, the one named last changes fastest.
Arguments:
- known_inverse: float32 [20480, 20480], P('row', 'col'), may hold values from -1.7818667 to 1.7818667, as said below
- first_panel: float32 [20480, 512], P('col', 'row'), may hold values from -1.25 to 1.25
- second_panel: float32 [20480, 512], P('col', 'row'), may hold values from -1.25 to 1.25
- coupling: float32 [512, 512], replicated, may hold values from -0.25 to 0.25
- first_diag: float32 [512, 512], replicated, may hold values from -6 to 6
- second_diag: float32 [512, 512], replicated, may hold values from -6 to 6
- first_present: int32 [160], replicated, may hold values 0 or 1
- second_present: int32 [160], replicated, may hold values 0 or 1
Outputs:
- first_block: float32 [20480, 512], P(('row', 'col'))
- first_inverse_diag: float32 [512, 512], P(None, 'col')
- second_block: float32 [20480, 512], P(('row', 'col'))
- second_cross: float32 [512, 512], P(None, 'col')
- second_inverse_diag: float32 [512, 512], P(None, 'col')
Inputs may be any that keep to these rules, and one draw needn't show every extreme that they name: known_inverse is exactly symmetric.
All inputs are finite; a program needn't handle non-finite values.
Results may differ from a plain program's by a relative error of at most 0.000098.
Values sent between devices are 32-bit elements; how exact they have to be, the bound alone decides.
A program may use at most 64 MiB of HBM per device.

v0:
```python
import jax
import jax.numpy as jnp
from jax import lax
from jax.sharding import PartitionSpec as P

BLK = 128


def spread(block, axis, holder):
    block = jnp.where(lax.axis_index(axis) == holder, block, jnp.zeros_like(block))
    return lax.psum(block, axis)


def product(left, right):
    return jnp.dot(left, right, precision=lax.Precision.HIGHEST, preferred_element_type=jnp.float32)


def transposed(left, right):
    return lax.dot_general(
        left,
        right,
        (((0,), (0,)), ((), ())),
        precision=lax.Precision.HIGHEST,
        preferred_element_type=jnp.float32,
    )


def masked(panel, present, col_index):
    row_total, col_total = panel.shape
    blocks = row_total // BLK
    local = lax.dynamic_slice_in_dim(present, col_index * blocks, blocks)
    shaped = panel.reshape(blocks, BLK, col_total) * local.astype(jnp.float32)[:, None, None]
    return shaped.reshape(row_total, col_total)


def piece_products(known_inverse, column_one, column_two, piece_one, piece_two, coupling):
    first_block = -lax.psum_scatter(
        product(known_inverse, column_one), "col", scatter_dimension=0, tiled=True
    )
    reached = lax.psum_scatter(
        product(known_inverse, column_two), "col", scatter_dimension=0, tiled=True
    )
    first_partial = transposed(piece_one, first_block)
    second_block = -(reached + product(first_block, coupling))
    cross_partial = transposed(first_block, piece_two)
    diag_partial = transposed(piece_two, second_block)
    return (first_block, second_block, first_partial, cross_partial, diag_partial)


def on_device(
    known_inverse,
    first_panel,
    second_panel,
    coupling,
    first_diag,
    second_diag,
    first_present,
    second_present,
):
    col_count = lax.axis_size("col")
    row_index = lax.axis_index("row")
    col_index = lax.axis_index("col")
    local_one = masked(first_panel, first_present, col_index)
    local_two = masked(second_panel, second_present, col_index)
    column_one, column_two = (
        lax.all_gather(local_one, "row", axis=1, tiled=True),
        lax.all_gather(local_two, "row", axis=1, tiled=True),
    )
    band_rows = known_inverse.shape[0]
    block_cols = known_inverse.shape[1]
    piece_rows = band_rows // col_count
    width_total = coupling.shape[0]
    owner = row_index * band_rows // block_cols
    offset = row_index * band_rows % block_cols
    own_start = col_index * piece_rows
    band_one = lax.dynamic_slice_in_dim(column_one, offset, band_rows)
    band_two = lax.dynamic_slice_in_dim(column_two, offset, band_rows)
    band_one, band_two = (spread(band_one, "col", owner), spread(band_two, "col", owner))
    piece_one = lax.dynamic_slice_in_dim(band_one, own_start, piece_rows)
    piece_two = lax.dynamic_slice_in_dim(band_two, own_start, piece_rows)
    first_block, second_block, first_partial, cross_partial, diag_partial = piece_products(
        known_inverse, column_one, column_two, piece_one, piece_two, coupling
    )
    col_width = width_total // col_count
    col_start = col_index * col_width
    first_sum = lax.psum(first_partial, ("row", "col"))
    first_inverse_diag = first_diag - first_sum
    cross_sum, diag_sum = lax.psum((cross_partial, diag_partial), ("row", "col"))
    second_cross = -(cross_sum + product(first_inverse_diag, coupling))
    second_inverse_diag = second_diag - diag_sum - transposed(coupling, second_cross)
    first_out = lax.dynamic_slice_in_dim(first_inverse_diag, col_start, col_width, 1)
    cross_out = lax.dynamic_slice_in_dim(second_cross, col_start, col_width, 1)
    second_out = lax.dynamic_slice_in_dim(second_inverse_diag, col_start, col_width, 1)
    return (first_block, first_out, second_block, cross_out, second_out)


def solution(mesh):
    in_specs = (P("row", "col"), P("col", "row"), P("col", "row"), P(), P(), P(), P(), P())
    out_specs = (
        P(("row", "col"), None),
        P(None, "col"),
        P(("row", "col"), None),
        P(None, "col"),
        P(None, "col"),
    )
    return jax.shard_map(
        on_device, mesh=mesh, in_specs=in_specs, out_specs=out_specs, check_vma=False
    )
```

profile of v0, /device:TPU:2, one launch (start us, length us, event | category | flops | bytes accessed | tf_op | source)
XLA Modules:
  0.0 611.4 jit_solution(1774505497310201889)
XLA Ops:
  7.2 0.9 dynamic-slice_convert_fusion
  8.2 1.6 broadcast_multiply_fusion.1
  9.9 1.6 broadcast_multiply_fusion
  11.6 66.8 %all-gather.3.cloned.1.call-done = f32[2560,512]{0,1:T(8,128)} async-done(((f32[2560,16]{0,1:T(8,128)}), f32[2560,512]{0,1:T(8,128)}) %all-gather.3.cloned.1.call-update) | async-done | bytes 5242896 | tf_op jit(solution)/shard_map/all_gather | solution.py:66
  78.4 15.7 %convolution_bitcast_fusion.1 = f32[640,512]{0,1:T(8,128)S(1)} fusion(f32[2560,512]{0,1:T(8,128)} %all-gather.3.cloned.1.call-done, f32[640,2560]{1,0:T(8,128)} %param.8), kind=kOutput, calls=%fused_computation.1 | convolution fusion | flops 10066329600 | bytes 13107200 | tf_op jit(solution)/shard_map/dot_general | solution.py:15
  94.1 1.5 copy.27
  95.7 2.9 dynamic-slice_select_fusion.1
  98.6 45.1 %all-gather.5.cloned.1.call-done = f32[2560,512]{0,1:T(8,128)} async-done(((f32[2560,16]{0,1:T(8,128)}), f32[2560,512]{0,1:T(8,128)}) %all-gather.5.cloned.1.call-update) | async-done | bytes 5242896 | tf_op jit(solution)/shard_map/all_gather | solution.py:67
  143.7 3.0 dynamic-slice_select_fusion
  146.7 0.2 reduce-scatter.9.cloned.1.call-start
  146.9 15.7 %convolution_bitcast_fusion = f32[640,512]{0,1:T(8,128)S(1)} fusion(f32[2560,512]{0,1:T(8,128)} %all-gather.5.cloned.1.call-done, f32[640,2560]{1,0:T(8,128)} %param.8), kind=kOutput, calls=%fused_computation | convolution fusion | flops 10066329600 | bytes 13107200 | tf_op jit(solution)/shard_map/dot_general | solution.py:15
  162.6 1.5 copy.29
  164.1 0.3 all-reduce.5.cloned.1.call-start
  164.4 19.8 %reduce-scatter.7.cloned.1.call-done = f32[80,512]{1,0:T(8,128)} async-done(((f32[640,512]{1,0:T(8,128)}), f32[80,512]{1,0:T(8,128)}) %reduce-scatter.7.cloned.1.call-update) | async-done | bytes 163856
  184.2 1.0 copy.28
  185.3 92.8 %all-reduce.7.cloned.1.call-done = (f32[640,512]{0,1:T(8,128)}, f32[640,512]{0,1:T(8,128)}) async-done(((f32[640,512]{0,1:T(8,128)}, f32[640,512]{0,1:T(8,128)}), (f32[640,512]{0,1:T(8,128)}, f32[640,512]{0,1:T(8,128)})) %all-reduce.7.cloned.1.call-update) | async-done | bytes 2621456 | tf_op jit(solution)/shard_map/psum | solution.py:11
  278.0 3.1 fusion.2
  281.2 3.1 fusion.6
  284.3 37.2 %reduce-scatter.9.cloned.1.call-done = f32[80,512]{1,0:T(8,128)} async-done(((f32[640,512]{1,0:T(8,128)}), f32[80,512]{1,0:T(8,128)}) %reduce-scatter.9.cloned.1.call-update) | async-done | bytes 163856 | tf_op jit(solution)/shard_map/reduce_scatter | solution.py:40
  321.5 1.6 fusion.1
  323.2 3.2 fusion.4
  326.4 1.2 constant_dynamic-slice_fusion
  327.7 0.8 copy.23
  328.5 267.3 %all-reduce.5.cloned.1.call-done = (f32[512,512]{1,0:T(8,128)}, f32[512,512]{1,0:T(8,128)}, f32[512,512]{0,1:T(8,128)}) async-done(((f32[512,512]{1,0:T(8,128)}, f32[512,512]{1,0:T(8,128)}, f32[512,512]{0,1:T(8,128)}), (f32[512,512]{1,0:T(8,128)}, f32[512,512]{1,0:T(8,128)}, f32[512,512]{0,1:T(8,128)})) %all-reduce.5.cloned.1.call-update) | async-done | bytes 3145744 | tf_op jit(solution)/shard_map/psum | solution.py:86
  595.9 1.5 sub.14
  597.4 0.1 constant_dynamic-slice_fusion.2
  597.5 1.8 fusion
  599.4 0.1 constant_dynamic-slice_fusion.1
  599.5 1.8 convolution_bitcast_fusion.2
  601.4 0.8 copy.24
  602.2 0.8 copy.25
  602.9 1.6 dynamic-slice_subtract_fusion
  (22 shorter events, 0.6 us)
Async XLA Ops:
  7.2 314.3 %copy-start = (f32[512,512]{1,0:T(8,128)S(1)}, f32[512,512]{1,0:T(8,128)}, u32[]{:S(2)}) copy-start(f32[512,512]{1,0:T(8,128)} %param.11) | copy-start | bytes 3145732
  7.2 71.2 %all-gather.3.cloned.1.call-start = ((), (), s32[]{:S(2)}) async-start(), calls=%async_computation.2 | async-start | bytes 5406720 | tf_op jit(solution)/shard_map/all_gather | solution.py:66
  9.8 133.9 %all-gather.5.cloned.1.call-start = ((), (), s32[]{:S(2)}) async-start(), calls=%async_computation.3 | async-start | bytes 5406720 | tf_op jit(solution)/shard_map/all_gather | solution.py:67
  11.5 172.7 %reduce-scatter.7.cloned.1.call-start = ((), (), s32[]{:S(2)}) async-start(), calls=%async_computation.4 | async-start | bytes 1474560
  95.6 182.4 %all-reduce.7.cloned.1.call-start = ((), (), s32[]{:S(2)}) async-start(), calls=%async_computation.7 | async-start | bytes 5242880 | tf_op jit(solution)/shard_map/psum | solution.py:11
  146.7 174.8 %reduce-scatter.9.cloned.1.call-start = ((), (), s32[]{:S(2)}) async-start(), calls=%async_computation.5 | async-start | bytes 1474560 | tf_op jit(solution)/shard_map/reduce_scatter | solution.py:40
  164.1 431.7 %all-reduce.5.cloned.1.call-start = ((), (), s32[]{:S(2)}) async-start(), calls=%async_computation.6 | async-start | bytes 6291456 | tf_op jit(solution)/shard_map/psum | solution.py:86
  323.1 3.2 copy-start.3
  326.4 269.5 %copy-start.1 = (f32[512,512]{1,0:T(8,128)S(1)}, f32[512,512]{1,0:T(8,128)}, u32[]{:S(2)}) copy-start(f32[512,512]{1,0:T(8,128)} %param.12) | copy-start | bytes 3145732
  595.9 1.7 copy-start.2
Sparse Core Ops, SparseCore 0:
  11.1 67.2 all-gather.2
  81.5 62.1 all-gather.4
  146.2 37.9 reduce-scatter.6
  186.8 91.2 all-reduce.6
  280.4 41.0 reduce-scatter.8
  327.1 268.6 all-reduce.4
where the time goes:
time: 612 us; the launch traced here: 611 us
  waiting for transfers between devices  529 us (86%)
  matrix products  46.2 us (8%)
  between operations  14.3 us (2%)
  other arithmetic  13.1 us (2%)
  local copies, waits for them, and re-layouts  8.01 us (1%)
    psum x1, waiting for transfers between devices, on_device(): first_sum = lax.psum(first_partial, ('row', 'col'))  267 us
    psum x1, waiting for transfers between devices, spread(): return lax.psum(block, axis)  92.8 us
    all_gather x1, waiting for transfers between devices, on_device(): lax.all_gather(local_one, 'row', axis=1, tiled=True)  66.8 us
    all_gather x1, waiting for transfers between devices, on_device(): lax.all_gather(local_two, 'row', axis=1, tiled=True)  45.1 us
    reduce_scatter x1, waiting for transfers between devices, piece_products(): lax.psum_scatter(product(known_inverse, column_two), 'col', scatter_dimen...  37.2 us
    dot_general x4, matrix products, product(): jnp.dot(left, right, precision=lax.Precision.HIGHEST, preferred_element_t...  35 us
    unnamed x7, waiting for transfers between devices  19.9 us
  transfers between devices with their start and end apart: 6, of which 6 were waited for; matrix products, arithmetic and copies ran while one was open for 8% of the time, Pallas kernels for 0%

commit v1 on v0

--- a/solution.py
+++ b/solution.py
@@ -8,7 +8,7 @@
 
 def spread(block, axis, holder):
     block = jnp.where(lax.axis_index(axis) == holder, block, jnp.zeros_like(block))
-    return lax.psum(block, axis)
+    return jnp.sum(lax.all_gather(block, axis), axis=0)
 
 
 def product(left, right):

time: 612 us -> 756 us (1.24)
  waiting for transfers between devices: 529 us -> 652 us
  local copies, waits for them, and re-layouts: 8.01 us -> 20.7 us
  other arithmetic: 13.1 us -> 21.7 us
    all_gather x0 -> x2, waiting for transfers between devices: none -> 211 us  [spread(): return jnp.sum(lax.all_gather(block, axis), axis=0)]
    psum x1 -> x0, waiting for transfers between devices: 92.8 us -> none  [spread(): return lax.psum(block, axis)]
    unnamed x15 -> x17, local copies, waits for them, and re-layouts: 6.43 us -> 19.1 us
    reduce_sum x0 -> x2, other arithmetic: none -> 8.68 us  [spread(): return jnp.sum(lax.all_gather(block, axis), axis=0)]
    unnamed x7 -> x8, waiting for transfers between devices: 19.9 us -> 17 us
  transfers between devices with their start and end apart: 6 -> 7, of which waited for: 6 -> 7; matrix products, arithmetic and copies ran while one was open for 8% -> 8% of each run, Pallas kernels for 0% -> 0%
where the time goes in v1:
time: 756 us
  waiting for transfers between devices  652 us (86%)
  matrix products  46.2 us (6%)
  other arithmetic  21.7 us (3%)
  local copies, waits for them, and re-layouts  20.7 us (3%)
  between operations  14.3 us (2%)
    psum x1, waiting for transfers between devices, on_device(): first_sum = lax.psum(first_partial, ('row', 'col'))  266 us
    all_gather x2, waiting for transfers between devices, spread(): return jnp.sum(lax.all_gather(block, axis), axis=0)  211 us
    all_gather x1, waiting for transfers between devices, on_device(): lax.all_gather(local_one, 'row', axis=1, tiled=True)  66.8 us
    all_gather x1, waiting for transfers between devices, on_device(): lax.all_gather(local_two, 'row', axis=1, tiled=True)  47.8 us
    reduce_scatter x1, waiting for transfers between devices, piece_products(): lax.psum_scatter(product(known_inverse, column_two), 'col', scatter_dimen...  43.1 us
    dot_general x4, matrix products, product(): jnp.dot(left, right, precision=lax.Precision.HIGHEST, preferred_element_t...  35 us
    unnamed x17, local copies, waits for them, and re-layouts  19.1 us
    unnamed x8, waiting for transfers between devices  17 us
  transfers between devices with their start and end apart: 7, of which 7 were waited for; matrix products, arithmetic and copies ran while one was open for 8% of the time, Pallas kernels for 0%

profile of v1, /device:TPU:2, one launch (start us, length us, event | category | flops | bytes accessed | tf_op | source)
XLA Modules:
  0.0 755.5 jit_solution(13563610552218058134)
XLA Ops:
  7.2 0.9 dynamic-slice_convert_fusion
  8.2 1.6 broadcast_multiply_fusion.1
  9.9 1.6 broadcast_multiply_fusion
  11.6 66.8 %all-gather.7.cloned.1.call-done = f32[2560,512]{0,1:T(8,128)} async-done(((f32[2560,16]{0,1:T(8,128)}), f32[2560,512]{0,1:T(8,128)}) %all-gather.7.cloned.1.call-update) | async-done | bytes 5242896 | tf_op jit(solution)/shard_map/all_gather | solution.py:66
  78.4 15.7 %convolution_bitcast_fusion.1 = f32[640,512]{0,1:T(8,128)S(1)} fusion(f32[2560,512]{0,1:T(8,128)} %all-gather.7.cloned.1.call-done, f32[640,2560]{1,0:T(8,128)} %param.8), kind=kOutput, calls=%fused_computation.3 | convolution fusion | flops 10066329600 | bytes 13107200 | tf_op jit(solution)/shard_map/dot_general | solution.py:15
  94.1 1.5 copy.27
  95.8 47.8 %all-gather.9.cloned.1.call-done = f32[2560,512]{0,1:T(8,128)} async-done(((f32[2560,16]{0,1:T(8,128)}), f32[2560,512]{0,1:T(8,128)}) %all-gather.9.cloned.1.call-update) | async-done | bytes 5242896 | tf_op jit(solution)/shard_map/all_gather | solution.py:67
  143.7 15.7 %convolution_bitcast_fusion = f32[640,512]{0,1:T(8,128)S(1)} fusion(f32[2560,512]{0,1:T(8,128)} %all-gather.9.cloned.1.call-done, f32[640,2560]{1,0:T(8,128)} %param.8), kind=kOutput, calls=%fused_computation.2 | convolution fusion | flops 10066329600 | bytes 13107200 | tf_op jit(solution)/shard_map/dot_general | solution.py:15
  159.4 1.6 copy.29
  161.1 2.9 dynamic-slice_select_fusion
  164.1 2.9 dynamic-slice_select_fusion.1
  167.3 16.9 %reduce-scatter.7.cloned.1.call-done = f32[80,512]{1,0:T(8,128)} async-done(((f32[640,512]{1,0:T(8,128)}), f32[80,512]{1,0:T(8,128)}) %reduce-scatter.7.cloned.1.call-update) | async-done | bytes 163856
  184.2 1.0 copy.28
  185.3 43.1 %reduce-scatter.9.cloned.1.call-done = f32[80,512]{1,0:T(8,128)} async-done(((f32[640,512]{1,0:T(8,128)}), f32[80,512]{1,0:T(8,128)}) %reduce-scatter.9.cloned.1.call-update) | async-done | bytes 163856 | tf_op jit(solution)/shard_map/reduce_scatter | solution.py:40
  228.3 1.6 fusion.1
  230.0 113.5 %all-gather.13.cloned.1.call-done = f32[5120,512]{0,1:T(8,128)} async-done(((f32[640,512]{0,1:T(8,128)}), f32[5120,512]{0,1:T(8,128)}) %all-gather.13.cloned.1.call-update) | async-done | bytes 10485776 | tf_op jit(solution)/shard_map/all_gather | solution.py:11
  343.5 6.3 copy.33
  349.7 4.2 bitcast_reduce_fusion
  353.9 3.2 fusion.4
  357.1 3.2 fusion.6
  360.3 97.7 %all-gather.11.cloned.1.call-done = f32[5120,512]{0,1:T(8,128)} async-done(((f32[640,512]{0,1:T(8,128)}), f32[5120,512]{0,1:T(8,128)}) %all-gather.11.cloned.1.call-update) | async-done | bytes 10485776 | tf_op jit(solution)/shard_map/all_gather | solution.py:11
  458.0 6.3 copy.32
  464.3 4.5 bitcast_reduce_fusion.1
  468.8 3.0 fusion.2
  471.8 1.2 constant_dynamic-slice_fusion
  473.1 0.8 copy.23
  473.9 266.1 %all-reduce.3.cloned.1.call-done = (f32[512,512]{1,0:T(8,128)}, f32[512,512]{1,0:T(8,128)}, f32[512,512]{0,1:T(8,128)}) async-done(((f32[512,512]{1,0:T(8,128)}, f32[512,512]{1,0:T(8,128)}, f32[512,512]{0,1:T(8,128)}), (f32[512,512]{1,0:T(8,128)}, f32[512,512]{1,0:T(8,128)}, f32[512,512]{0,1:T(8,128)})) %all-reduce.3.cloned.1.call-update) | async-done | bytes 3145744 | tf_op jit(solution)/shard_map/psum | solution.py:86
  740.0 1.5 sub.14
  741.5 1.8 fusion
  743.4 1.8 convolution_bitcast_fusion.2
  745.5 0.8 copy.25
  747.1 1.6 dynamic-slice_subtract_fusion
  (29 shorter events, 2.2 us)
Async XLA Ops:
  7.2 221.2 %copy-start = (f32[512,512]{1,0:T(8,128)S(1)}, f32[512,512]{1,0:T(8,128)}, u32[]{:S(2)}) copy-start(f32[512,512]{1,0:T(8,128)} %param.11) | copy-start | bytes 3145732
  7.2 71.2 %all-gather.7.cloned.1.call-start = ((), (), s32[]{:S(2)}) async-start(), calls=%async_computation.2 | async-start | bytes 5406720 | tf_op jit(solution)/shard_map/all_gather | solution.py:66
  9.8 133.9 %all-gather.9.cloned.1.call-start = ((), (), s32[]{:S(2)}) async-start(), calls=%async_computation.3 | async-start | bytes 5406720 | tf_op jit(solution)/shard_map/all_gather | solution.py:67
  11.5 172.7 %reduce-scatter.7.cloned.1.call-start = ((), (), s32[]{:S(2)}) async-start(), calls=%async_computation.6 | async-start | bytes 1474560
  95.6 132.7 %reduce-scatter.9.cloned.1.call-start = ((), (), s32[]{:S(2)}) async-start(), calls=%async_computation.7 | async-start | bytes 1474560 | tf_op jit(solution)/shard_map/reduce_scatter | solution.py:40
  161.0 182.4 %all-gather.13.cloned.1.call-start = ((), (), s32[]{:S(2)}) async-start(), calls=%async_computation.5 | async-start | bytes 11796480 | tf_op jit(solution)/shard_map/all_gather | solution.py:11
  164.0 294.0 %all-gather.11.cloned.1.call-start = ((), (), s32[]{:S(2)}) async-start(), calls=%async_computation.4 | async-start | bytes 11796480 | tf_op jit(solution)/shard_map/all_gather | solution.py:11
  167.0 572.9 %all-reduce.3.cloned.1.call-start = ((), (), s32[]{:S(2)}) async-start(), calls=%async_computation.8 | async-start | bytes 6291456 | tf_op jit(solution)/shard_map/psum | solution.py:86
  230.0 124.0 %copy-start.3 = (f32[80,512]{1,0:T(8,128)}, f32[80,512]{1,0:T(8,128)S(1)}, u32[]{:S(2)}) copy-start(f32[80,512]{1,0:T(8,128)S(1)} %fusion.1) | copy-start | bytes 491524
  471.8 268.2 %copy-start.1 = (f32[512,512]{1,0:T(8,128)S(1)}, f32[512,512]{1,0:T(8,128)}, u32[]{:S(2)}) copy-start(f32[512,512]{1,0:T(8,128)} %param.12) | copy-start | bytes 3145732
  740.0 1.5 copy-start.2
Sparse Core Ops, SparseCore 0:
  11.1 67.2 all-gather.6
  81.5 62.1 all-gather.8
  146.2 37.9 reduce-scatter.6
  186.6 41.6 reduce-scatter.8
  230.0 113.4 all-gather.12
  345.1 112.8 all-gather.10
  471.9 268.0 all-reduce.2
